TPU v7x, 32 devices: a whole 2x2x4 slice. The times are simulated.
32 devices in a mesh: blk: 4 (over y, x), rep: 8 (over z, core).
Axes of the slice: x: 2, y: 2, z: 4, core: 2. Of those that a mesh axis runs over, the one named last changes fastest.
Arguments:
- query_hidden: bfloat16 [8, 16, 32, 768], P('rep', 'blk'), may hold values from -18 to 18
- passage_hidden: bfloat16 [8, 16, 512, 768], P('rep', 'blk'), may hold values from -6 to 6
- lengths: int32 [8, 16], P('rep', 'blk'), may hold values from 64 to 512
- projection: bfloat16 [768, 128], replicated, may hold values from -0.21875 to 0.21875
Outputs:
- query_grad: float32 [8, 16, 32, 128], P('rep', 'blk')
- passage_grad: float32 [8, 16, 512, 128], P('rep', 'blk')
- grad_weight: float32 [768, 128], replicated
- loss: float32 [], replicated
All inputs are finite; a program needn't handle non-finite values.
Results may differ from a plain program's by a relative error of at most 0.0097.
Values may be sent and summed in bfloat16 or wider, within the bound.
A program may use at most 128 MiB of HBM per device.

v0:
```python
import jax
import jax.numpy as jnp
from jax import lax
from jax.sharding import PartitionSpec as P

temper = 0.5


def soft_scores(scores, lens):
    slots = scores.shape[-1]
    valid = lax.broadcasted_iota(jnp.int32, (lens.shape[0], slots), 1) < lens[:, None]
    scaled = jnp.where(valid[None], scores / temper, -jnp.inf)
    top = jnp.max(scaled, -1, keepdims=True)
    logz = top + jnp.log(jnp.sum(jnp.exp(scaled - top), -1, keepdims=True))
    pooled = temper * (logz[..., 0] - jnp.log(lens.astype(jnp.float32))[None])
    return (pooled, scaled, logz)


def cross_entropy(score, first, total):
    top = jnp.max(score, 1, keepdims=True)
    lse = top + jnp.log(jnp.sum(jnp.exp(score - top), 1, keepdims=True))
    target = lax.broadcasted_iota(jnp.int32, score.shape, 1) == first + lax.broadcasted_iota(
        jnp.int32, score.shape, 0
    )
    loss_part = jnp.sum(lse[:, 0] - jnp.sum(jnp.where(target, score, 0.0), 1))
    dscore = (jnp.exp(score - lse) - target.astype(jnp.float32)) / total
    return (loss_part, dscore)


def weighted(dscore, scaled, logz, qlen):
    spread = jnp.repeat(dscore, qlen, axis=0)
    grad_a = (spread[:, :, None] * jnp.exp(scaled - logz)).astype(jnp.bfloat16)
    return grad_a.reshape(grad_a.shape[0], -1)


def shards(query_hidden, passage_hidden, lengths, projection):
    hidden = projection.shape[0]
    nquery = query_hidden.shape[1]
    qlen = query_hidden.shape[2]
    npass = passage_hidden.shape[1]
    plen = passage_hidden.shape[2]
    groups = lax.axis_size("blk")
    total = groups * lax.axis_size("rep") * nquery
    first = lax.axis_index("blk") * nquery
    qflat = query_hidden[0].reshape(-1, hidden)
    pflat = passage_hidden[0].reshape(-1, hidden)
    qtok = jnp.dot(qflat, projection, preferred_element_type=jnp.float32).astype(jnp.bfloat16)
    ptok = jnp.dot(pflat, projection, preferred_element_type=jnp.float32).astype(jnp.bfloat16)
    every_tok = lax.all_gather(qtok, "blk", axis=0, tiled=True)
    scores = jnp.dot(every_tok, ptok.T, preferred_element_type=jnp.float32).reshape(
        groups * nquery * qlen, npass, plen
    )
    pooled, scaled, logz = soft_scores(scores, lengths[0])
    block_score = jnp.sum(pooled.reshape(groups * nquery, qlen, npass), 1)
    score = lax.all_to_all(block_score, "blk", split_axis=0, concat_axis=1, tiled=True)
    loss_part, dscore = cross_entropy(score, first, total)
    block_grad = lax.all_to_all(dscore, "blk", split_axis=1, concat_axis=0, tiled=True)
    grad_a = weighted(block_grad, scaled, logz, qlen)
    pgrad = jnp.dot(grad_a.T, every_tok, preferred_element_type=jnp.float32)
    qgrad = lax.psum_scatter(
        jnp.dot(grad_a, ptok, preferred_element_type=jnp.float32),
        "blk",
        scatter_dimension=0,
        tiled=True,
    )
    wgrad = jnp.dot(qflat.T, qgrad.astype(jnp.bfloat16), preferred_element_type=jnp.float32)
    wgrad = wgrad + jnp.dot(pflat.T, pgrad.astype(jnp.bfloat16), preferred_element_type=jnp.float32)
    wgrad, loss_sum = lax.psum((wgrad, loss_part), ("blk", "rep"))
    query_grad = qgrad.reshape(1, nquery, qlen, -1)
    passage_grad = pgrad.reshape(1, npass, plen, -1)
    return (query_grad, passage_grad, wgrad, loss_sum / total)


def solution(mesh):
    return jax.shard_map(
        shards,
        mesh=mesh,
        in_specs=(P("rep", "blk", None, None), P("rep", "blk", None, None), P("rep", "blk"), P()),
        out_specs=(P("rep", "blk", None, None), P("rep", "blk", None, None), P(), P()),
        check_vma=False,
    )
```

profile of v0, /device:TPU:0, one launch (start us, length us, event | category | flops | bytes accessed | tf_op | source)
XLA Modules:
  0.0 233.2 jit_solution(2799079594073589666)
XLA Ops:
  7.2 1.9 copy-done
  9.1 1.9 convolution_convert_fusion
  11.0 0.2 convolution_convert_fusion.1
  11.2 9.9 %all_gather.3 = bf16[512,128]{1,0:T(8,128)(2,1)S(1)} all-gather(bf16[128,128]{1,0:T(8,128)(2,1)S(1)} %convolution_convert_fusion.1), channel_id=1, replica_groups=mesh['blk'=4,'rep'=8] {'blk'}, dimensions={0}, use_global_device_ids=true | all-gather | bytes 163840 | tf_op jit(solution)/shard_map/all_gather | solution.py:49
  21.2 2.6 %convolution_multiply_fusion = f32[512,2048]{1,0:T(8,128)} fusion(bf16[512,128]{1,0:T(8,128)(2,1)S(1)} %all_gather.3, bf16[2048,128]{1,0:T(8,128)(2,1)S(1)} %convolution_convert_fusion), kind=kOutput, calls=%fused_computation.3 | convolution fusion | flops 269484032 | bytes 4849664 | tf_op jit(solution)/shard_map/dot_general | solution.py:50
  23.8 6.0 %div.19 = f32[512,4,512]{2,1,0:T(4,128)} reshape(f32[512,2048]{1,0:T(8,128)} %convolution_multiply_fusion) | data formatting | bytes 8388608 | tf_op jit(solution)/shard_map/div | solution.py:12
  29.9 3.3 %select_reduce_fusion = f32[512,4]{1,0:T(8,128)S(1)} fusion(f32[512,4,512]{2,1,0:T(4,128)} %div.19, pred[4,512]{1,0:T(4,128)(4,1)S(1)} %iota_compare_fusion), kind=kLoop, calls=%fused_computation.2 | loop fusion | flops 2095104 | bytes 4204544 | tf_op jit(solution)/shard_map/reduce_max | solution.py:13
  33.3 2.6 %exponential_reduce_fusion = f32[512,4]{1,0:T(8,128)S(1)} fusion(f32[512,4,512]{2,1,0:T(4,128)S(1)} %copy-done.1, f32[512,4]{1,0:T(8,128)S(1)} %select_reduce_fusion, pred[4,512]{1,0:T(4,128)(4,1)S(1)} %iota_compare_fusion), kind=kLoop, calls=%fused_computation.1 | loop fusion | flops 3143680 | bytes 4212736 | tf_op jit(solution)/shard_map/reduce_sum | solution.py:14
  36.0 0.7 copy.11
  36.7 3.2 %all-to-all-start = ((f32[4,4,4]{1,2,0:T(4,128)}), f32[4,4,4]{1,2,0:T(4,128)S(1)}, u32[]{:S(2)}, u32[]{:S(2)}) async-start(f32[4,4,4]{1,2,0:T(4,128)} %copy.11), calls=%async_computation | async-start | bytes 16384 | tf_op jit(solution)/shard_map/all_to_all | solution.py:55
  40.0 0.6 multiply_add_fusion
  40.5 0.5 iota_add_fusion
  41.1 0.7 sub.65
  41.8 3.9 %copy.21 = f32[64,8,4,512]{3,1,2,0:T(8,128)} copy(f32[64,8,4,512]{3,2,1,0:T(4,128)S(1)} %bitcast.49) | data formatting | bytes 8388608
  45.8 0.6 subtract_reduce_fusion
  46.5 0.7 fusion.5
  47.1 4.2 %all-to-all-start.1 = ((f32[4,4,4]{0,2,1:T(4,128)}), f32[4,4,4]{0,2,1:T(4,128)S(1)}, u32[]{:S(2)}, u32[]{:S(2)}) async-start(f32[4,4,4]{0,2,1:T(4,128)} %fusion.5), calls=%async_computation.1 | async-start | bytes 16384 | tf_op jit(solution)/shard_map/all_to_all | solution.py:57
  51.4 4.6 %all-to-all-done.1 = f32[4,4,4]{0,2,1:T(4,128)S(1)} async-done(((f32[4,4,4]{0,2,1:T(4,128)}), f32[4,4,4]{0,2,1:T(4,128)S(1)}, u32[]{:S(2)}, u32[]{:S(2)}) %all-to-all-start.1) | async-done | bytes 288 | tf_op jit(solution)/shard_map/all_to_all | solution.py:57
  56.1 0.7 mul.27
  56.9 2.0 copy.19
  59.0 1.3 copy-done.4
  60.3 1.6 multiply_convert_fusion
  61.9 1.3 copy-done.3
  63.2 1.4 fusion.10
  64.7 2.3 fusion.11
  67.0 1.0 copy-done.5
  68.0 0.6 fusion.1
  68.6 19.9 %reduce-scatter.2.cloned.1.call-done = f32[128,128]{1,0:T(8,128)} async-done(((f32[512,128]{1,0:T(8,128)}), f32[128,128]{1,0:T(8,128)}) %reduce-scatter.2.cloned.1.call-update) | async-done | bytes 65552 | tf_op jit(solution)/shard_map/reduce_scatter | solution.py:60
  88.5 1.9 fusion
  90.5 39.6 %psum.15 = f32[]{:T(128)} all-reduce(f32[]{:T(128)} %get-tuple-element.14), channel_id=1, replica_groups=mesh['blk'=4,'rep'=8] {'blk','rep'}, use_global_device_ids=true, to_apply=%region_9.10 | all-reduce | flops 1 | bytes 8 | tf_op jit(solution)/shard_map/psum | solution.py:68
  130.7 92.6 %all-reduce.2.cloned.1.call-done = f32[768,128]{0,1:T(8,128)} async-done(((f32[768,128]{0,1:T(8,128)}), f32[768,128]{0,1:T(8,128)}) %all-reduce.2.cloned.1.call-update) | async-done | bytes 393232 | tf_op jit(solution)/shard_map/psum | solution.py:68
  223.3 1.9 copy.14
  (40 shorter events, 0.9 us)
Async XLA Ops:
  7.2 1.9 copy-start
  7.2 3.8 %copy-start.8 = (bf16[768,128]{1,0:T(8,128)(2,1)S(1)}, bf16[768,128]{1,0:T(8,128)(2,1)}, u32[]{:S(2)}) copy-start(bf16[768,128]{1,0:T(8,128)(2,1)} %param.7) | copy-start | bytes 589828
  7.2 3.8 %copy-start.9 = (bf16[1,4,32,768]{3,2,1,0:T(8,128)(2,1)S(1)}, bf16[1,4,32,768]{3,2,1,0:T(8,128)(2,1)}, u32[]{:S(2)}) copy-start(bf16[1,4,32,768]{3,2,1,0:T(8,128)(2,1)} %param.4) | copy-start | bytes 589828
  11.0 10.2 %copy-start.6 = (bf16[2048,128]{1,0:T(8,128)(2,1)}, bf16[2048,128]{1,0:T(8,128)(2,1)S(1)}, u32[]{:S(2)}) copy-start(bf16[2048,128]{1,0:T(8,128)(2,1)S(1)} %convolution_convert_fusion) | copy-start | bytes 1572868
  23.8 6.0 %copy-start.11 = (s32[1,4]{1,0:T(1,128)S(1)}, s32[1,4]{1,0:T(1,128)}, u32[]{:S(2)}) copy-start(s32[1,4]{1,0:T(1,128)} %param.6) | copy-start | bytes 52
  29.8 3.4 %copy-start.1 = (f32[512,4,512]{2,1,0:T(4,128)S(1)}, f32[512,4,512]{2,1,0:T(4,128)}, u32[]{:S(2)}) copy-start(f32[512,4,512]{2,1,0:T(4,128)} %div.19) | copy-start | bytes 12582916
  36.7 9.0 %all-to-all-start = ((f32[4,4,4]{1,2,0:T(4,128)}), f32[4,4,4]{1,2,0:T(4,128)S(1)}, u32[]{:S(2)}, u32[]{:S(2)}) async-start(f32[4,4,4]{1,2,0:T(4,128)} %copy.11), calls=%async_computation | async-start | bytes 16384 | tf_op jit(solution)/shard_map/all_to_all | solution.py:55
  41.8 4.0 %copy-start.10 = (s32[4,4]{1,0:T(4,128)S(1)}, s32[4,4]{1,0:T(4,128)}, u32[]{:S(2)}) copy-start(s32[4,4]{1,0:T(4,128)} %multiply_add_fusion) | copy-start | bytes 196
  41.8 4.0 %copy-start.13 = (s32[4]{0:T(128)S(1)}, s32[4]{0:T(128)}, u32[]{:S(2)}) copy-start(s32[4]{0:T(128)} %iota_add_fusion) | copy-start | bytes 52
  41.8 9.5 %copy-start.12 = (s32[1,4]{1,0:T(1,128)S(1)}, s32[1,4]{1,0:T(1,128)}, u32[]{:S(2)}) copy-start(s32[1,4]{1,0:T(1,128)} %param.6) | copy-start | bytes 52
  47.1 8.8 %all-to-all-start.1 = ((f32[4,4,4]{0,2,1:T(4,128)}), f32[4,4,4]{0,2,1:T(4,128)S(1)}, u32[]{:S(2)}, u32[]{:S(2)}) async-start(f32[4,4,4]{0,2,1:T(4,128)} %fusion.5), calls=%async_computation.1 | async-start | bytes 16384 | tf_op jit(solution)/shard_map/all_to_all | solution.py:57
  51.3 37.2 %reduce-scatter.2.cloned.1.call-start = ((), (), s32[]{:S(2)}) async-start(), calls=%async_computation.3 | async-start | bytes 327680 | tf_op jit(solution)/shard_map/reduce_scatter | solution.py:60
  56.8 2.2 copy-start.2
  56.8 3.5 %copy-start.4 = (f32[64,8,4,512]{3,1,2,0:T(8,128)S(1)}, f32[64,8,4,512]{3,1,2,0:T(8,128)}, u32[]{:S(2)}) copy-start(f32[64,8,4,512]{3,1,2,0:T(8,128)} %copy.21) | copy-start | bytes 12582916
  60.3 2.9 %copy-start.7 = (bf16[2048,128]{1,0:T(8,128)(2,1)S(1)}, bf16[2048,128]{1,0:T(8,128)(2,1)}, u32[]{:S(2)}) copy-start(bf16[2048,128]{1,0:T(8,128)(2,1)} %copy-done.6) | copy-start | bytes 1572868
  61.9 1.4 copy-start.3
  64.7 158.7 %all-reduce.2.cloned.1.call-start = ((), (), s32[]{:S(2)}) async-start(), calls=%async_computation.4 | async-start | bytes 786432 | tf_op jit(solution)/shard_map/psum | solution.py:68
  67.0 1.0 copy-start.5
Sparse Core Ops, SparseCore 0:
  64.8 23.6 reduce-scatter.1
  94.4 128.9 all-reduce.1
where the time goes:
time: 234 us; the launch traced here: 233 us
  waiting for transfers between devices  117 us (50%)
  blocking collectives  49.5 us (21%)
  local copies, waits for them, and re-layouts  21.9 us (9%)
  between operations  16 us (7%)
  matrix products  11 us (5%)
  other arithmetic  10.1 us (4%)
  starting transfers between devices  7.45 us (3%)
    psum x1, waiting for transfers between devices, shards(): wgrad, loss_sum = lax.psum((wgrad, loss_part), ('blk', 'rep'))  92.6 us
    psum x1, blocking collectives, shards(): wgrad, loss_sum = lax.psum((wgrad, loss_part), ('blk', 'rep'))  39.6 us
    reduce_scatter x1, waiting for transfers between devices, shards(): lax.psum_scatter(jnp.dot(grad_a, ptok, preferred_element_type=jnp.float32...  19.9 us
    unnamed x33, local copies, waits for them, and re-layouts  13.6 us
    all_gather x1, blocking collectives, shards(): every_tok = lax.all_gather(qtok, 'blk', axis=0, tiled=True)  9.94 us
    div x1, local copies, waits for them, and re-layouts, soft_scores(): scaled = jnp.where(valid[None], scores / temper, -jnp.inf)  6.03 us
  transfers between devices with their start and end apart: 4, of which 3 were waited for; matrix products, arithmetic and copies ran while one was open for 4% of the time, Pallas kernels for 0%

commit v1 on v0

--- a/solution.py
+++ b/solution.py
@@ -65,7 +65,7 @@
     )
     wgrad = jnp.dot(qflat.T, qgrad.astype(jnp.bfloat16), preferred_element_type=jnp.float32)
     wgrad = wgrad + jnp.dot(pflat.T, pgrad.astype(jnp.bfloat16), preferred_element_type=jnp.float32)
-    wgrad, loss_sum = lax.psum((wgrad, loss_part), ("blk", "rep"))
+    wgrad, loss_sum = lax.psum(lax.psum((wgrad, loss_part), axis_name="rep"), axis_name="blk")
     query_grad = qgrad.reshape(1, nquery, qlen, -1)
     passage_grad = pgrad.reshape(1, npass, plen, -1)
     return (query_grad, passage_grad, wgrad, loss_sum / total)

time: 234 us -> 204 us (0.87)
  waiting for transfers between devices: 117 us -> 102 us
  blocking collectives: 49.5 us -> 34.7 us
    psum x1 -> x2, waiting for transfers between devices: 92.6 us -> 77.5 us  [the longest x1 56.8 us: shards(): lax.psum((wgrad, loss_part), axis_name='rep')]
    psum x1 -> x2, blocking collectives: 39.6 us -> 24.8 us  [the longest x1 14.3 us: shards(): lax.psum((wgrad, loss_part), axis_name='rep')]
  transfers between devices with their start and end apart: 4 -> 5, of which waited for: 3 -> 4; matrix products, arithmetic and copies ran while one was open for 4% -> 4% of each run, Pallas kernels for 0% -> 0%
where the time goes in v1:
time: 204 us; the launch traced here: 203 us
  waiting for transfers between devices  102 us (50%)
  blocking collectives  34.7 us (17%)
  local copies, waits for them, and re-layouts  21.9 us (11%)
  between operations  15.7 us (8%)
  matrix products  11 us (5%)
  other arithmetic  10.1 us (5%)
  starting transfers between devices  7.49 us (4%)
    psum x1, waiting for transfers between devices, shards(): lax.psum((wgrad, loss_part), axis_name='rep')  56.8 us
    psum x1, waiting for transfers between devices, shards(): lax.psum(lax.psum((wgrad, loss_part), axis_name='rep'), axis_name='blk')  20.7 us
    reduce_scatter x1, waiting for transfers between devices, shards(): lax.psum_scatter(jnp.dot(grad_a, ptok, preferred_element_type=jnp.float32...  19.9 us
    psum x1, blocking collectives, shards(): lax.psum((wgrad, loss_part), axis_name='rep')  14.3 us
    unnamed x33, local copies, waits for them, and re-layouts  13.6 us
    psum x1, blocking collectives, shards(): lax.psum(lax.psum((wgrad, loss_part), axis_name='rep'), axis_name='blk')  10.4 us
    all_gather x1, blocking collectives, shards(): every_tok = lax.all_gather(qtok, 'blk', axis=0, tiled=True)  9.94 us
    div x1, local copies, waits for them, and re-layouts, soft_scores(): scaled = jnp.where(valid[None], scores / temper, -jnp.inf)  6.03 us
  transfers between devices with their start and end apart: 5, of which 4 were waited for; matrix products, arithmetic and copies ran while one was open for 4% of the time, Pallas kernels for 0%

profile of v1, /device:TPU:0, one launch (start us, length us, event | category | flops | bytes accessed | tf_op | source)
XLA Modules:
  0.0 203.1 jit_solution(9297494452505017876)
XLA Ops:
  7.2 1.9 copy-done
  9.1 1.9 convolution_convert_fusion
  11.2 9.9 %all_gather.3 = bf16[512,128]{1,0:T(8,128)(2,1)S(1)} all-gather(bf16[128,128]{1,0:T(8,128)(2,1)S(1)} %convolution_convert_fusion.1), channel_id=1, replica_groups=mesh['blk'=4,'rep'=8] {'blk'}, dimensions={0}, use_global_device_ids=true | all-gather | bytes 163840 | tf_op jit(solution)/shard_map/all_gather | solution.py:49
  21.2 2.6 %convolution_multiply_fusion = f32[512,2048]{1,0:T(8,128)} fusion(bf16[512,128]{1,0:T(8,128)(2,1)S(1)} %all_gather.3, bf16[2048,128]{1,0:T(8,128)(2,1)S(1)} %convolution_convert_fusion), kind=kOutput, calls=%fused_computation.3 | convolution fusion | flops 269484032 | bytes 4849664 | tf_op jit(solution)/shard_map/dot_general | solution.py:50
  23.8 6.0 %div.19 = f32[512,4,512]{2,1,0:T(4,128)} reshape(f32[512,2048]{1,0:T(8,128)} %convolution_multiply_fusion) | data formatting | bytes 8388608 | tf_op jit(solution)/shard_map/div | solution.py:12
  29.9 3.3 %select_reduce_fusion = f32[512,4]{1,0:T(8,128)S(1)} fusion(f32[512,4,512]{2,1,0:T(4,128)} %div.19, pred[4,512]{1,0:T(4,128)(4,1)S(1)} %iota_compare_fusion), kind=kLoop, calls=%fused_computation.2 | loop fusion | flops 2095104 | bytes 4204544 | tf_op jit(solution)/shard_map/reduce_max | solution.py:13
  33.3 2.6 %exponential_reduce_fusion = f32[512,4]{1,0:T(8,128)S(1)} fusion(f32[512,4,512]{2,1,0:T(4,128)S(1)} %copy-done.1, f32[512,4]{1,0:T(8,128)S(1)} %select_reduce_fusion, pred[4,512]{1,0:T(4,128)(4,1)S(1)} %iota_compare_fusion), kind=kLoop, calls=%fused_computation.1 | loop fusion | flops 3143680 | bytes 4212736 | tf_op jit(solution)/shard_map/reduce_sum | solution.py:14
  36.0 0.7 copy.11
  36.7 3.2 %all-to-all-start = ((f32[4,4,4]{1,2,0:T(4,128)}), f32[4,4,4]{1,2,0:T(4,128)S(1)}, u32[]{:S(2)}, u32[]{:S(2)}) async-start(f32[4,4,4]{1,2,0:T(4,128)} %copy.11), calls=%async_computation | async-start | bytes 16384 | tf_op jit(solution)/shard_map/all_to_all | solution.py:55
  40.0 0.6 multiply_add_fusion
  41.1 0.7 sub.65
  41.8 3.9 %copy.21 = f32[64,8,4,512]{3,1,2,0:T(8,128)} copy(f32[64,8,4,512]{3,2,1,0:T(4,128)S(1)} %bitcast.49) | data formatting | bytes 8388608
  45.8 0.6 subtract_reduce_fusion
  46.5 0.7 fusion.5
  47.1 4.2 %all-to-all-start.1 = ((f32[4,4,4]{0,2,1:T(4,128)}), f32[4,4,4]{0,2,1:T(4,128)S(1)}, u32[]{:S(2)}, u32[]{:S(2)}) async-start(f32[4,4,4]{0,2,1:T(4,128)} %fusion.5), calls=%async_computation.1 | async-start | bytes 16384 | tf_op jit(solution)/shard_map/all_to_all | solution.py:57
  51.4 4.6 %all-to-all-done.1 = f32[4,4,4]{0,2,1:T(4,128)S(1)} async-done(((f32[4,4,4]{0,2,1:T(4,128)}), f32[4,4,4]{0,2,1:T(4,128)S(1)}, u32[]{:S(2)}, u32[]{:S(2)}) %all-to-all-start.1) | async-done | bytes 288 | tf_op jit(solution)/shard_map/all_to_all | solution.py:57
  56.1 0.7 mul.27
  56.9 2.0 %copy.19 = f32[64,8,4,512]{3,1,2,0:T(8,128)S(1)} copy(f32[64,8,4,512]{3,2,1,0:T(4,128)S(1)} %bitcast.50) | data formatting | bytes 8388608
  59.0 1.3 copy-done.4
  60.3 1.6 multiply_convert_fusion
  61.9 1.3 copy-done.3
  63.2 1.4 fusion.10
  64.7 2.3 %fusion.11 = f32[2048,128]{1,0:T(8,128)S(1)} fusion(bf16[512,2048]{1,0:T(8,128)(2,1)} %copy-done.3, bf16[512,128]{1,0:T(8,128)(2,1)S(1)} %all_gather.3), kind=kOutput, calls=%fused_computation.31 | convolution fusion | flops 268435456 | bytes 3276800 | tf_op jit(solution)/shard_map/dot_general | solution.py:59
  67.0 1.0 copy-done.5
  68.0 0.6 fusion.1
  68.6 19.9 %reduce-scatter.2.cloned.1.call-done = f32[128,128]{1,0:T(8,128)} async-done(((f32[512,128]{1,0:T(8,128)}), f32[128,128]{1,0:T(8,128)}) %reduce-scatter.2.cloned.1.call-update) | async-done | bytes 65552 | tf_op jit(solution)/shard_map/reduce_scatter | solution.py:60
  88.5 1.9 fusion
  90.5 56.8 %all-reduce.3.cloned.1.call-done = f32[768,128]{0,1:T(8,128)} async-done(((f32[768,128]{0,1:T(8,128)}), f32[768,128]{0,1:T(8,128)}) %all-reduce.3.cloned.1.call-update) | async-done | bytes 393232 | tf_op jit(solution)/shard_map/psum | solution.py:68
  147.4 14.3 %psum.30 = f32[]{:T(128)} all-reduce(f32[]{:T(128)} %get-tuple-element.14), channel_id=1, replica_groups=mesh['blk'=4,'rep'=8] {'rep'}, use_global_device_ids=true, to_apply=%region_10.11 | all-reduce | flops 1 | bytes 8 | tf_op jit(solution)/shard_map/psum | solution.py:68
  161.7 10.4 %psum.31 = f32[]{:T(128)} all-reduce(f32[]{:T(128)} %psum.30), channel_id=1, replica_groups=mesh['blk'=4,'rep'=8] {'blk'}, use_global_device_ids=true, to_apply=%region_11.12 | all-reduce | flops 1 | bytes 8 | tf_op jit(solution)/shard_map/psum | solution.py:68
  172.8 20.7 %all-reduce.5.cloned.1.call-done = f32[768,128]{0,1:T(8,128)} async-done(((f32[768,128]{0,1:T(8,128)}), f32[768,128]{0,1:T(8,128)}) %all-reduce.5.cloned.1.call-update) | async-done | bytes 393232 | tf_op jit(solution)/shard_map/psum | solution.py:68
  193.5 1.9 copy.14
  (44 shorter events, 1.6 us)
Async XLA Ops:
  7.2 1.9 copy-start
  7.2 3.8 %copy-start.8 = (bf16[768,128]{1,0:T(8,128)(2,1)S(1)}, bf16[768,128]{1,0:T(8,128)(2,1)}, u32[]{:S(2)}) copy-start(bf16[768,128]{1,0:T(8,128)(2,1)} %param.7) | copy-start | bytes 589828
  7.2 3.8 %copy-start.9 = (bf16[1,4,32,768]{3,2,1,0:T(8,128)(2,1)S(1)}, bf16[1,4,32,768]{3,2,1,0:T(8,128)(2,1)}, u32[]{:S(2)}) copy-start(bf16[1,4,32,768]{3,2,1,0:T(8,128)(2,1)} %param.4) | copy-start | bytes 589828
  11.0 10.2 %copy-start.6 = (bf16[2048,128]{1,0:T(8,128)(2,1)}, bf16[2048,128]{1,0:T(8,128)(2,1)S(1)}, u32[]{:S(2)}) copy-start(bf16[2048,128]{1,0:T(8,128)(2,1)S(1)} %convolution_convert_fusion) | copy-start | bytes 1572868
  23.8 6.0 %copy-start.11 = (s32[1,4]{1,0:T(1,128)S(1)}, s32[1,4]{1,0:T(1,128)}, u32[]{:S(2)}) copy-start(s32[1,4]{1,0:T(1,128)} %param.6) | copy-start | bytes 52
  29.8 3.4 %copy-start.1 = (f32[512,4,512]{2,1,0:T(4,128)S(1)}, f32[512,4,512]{2,1,0:T(4,128)}, u32[]{:S(2)}) copy-start(f32[512,4,512]{2,1,0:T(4,128)} %div.19) | copy-start | bytes 12582916
  36.7 9.0 %all-to-all-start = ((f32[4,4,4]{1,2,0:T(4,128)}), f32[4,4,4]{1,2,0:T(4,128)S(1)}, u32[]{:S(2)}, u32[]{:S(2)}) async-start(f32[4,4,4]{1,2,0:T(4,128)} %copy.11), calls=%async_computation | async-start | bytes 16384 | tf_op jit(solution)/shard_map/all_to_all | solution.py:55
  41.8 4.0 %copy-start.10 = (s32[4,4]{1,0:T(4,128)S(1)}, s32[4,4]{1,0:T(4,128)}, u32[]{:S(2)}) copy-start(s32[4,4]{1,0:T(4,128)} %multiply_add_fusion) | copy-start | bytes 196
  41.8 4.0 %copy-start.13 = (s32[4]{0:T(128)S(1)}, s32[4]{0:T(128)}, u32[]{:S(2)}) copy-start(s32[4]{0:T(128)} %iota_add_fusion) | copy-start | bytes 52
  41.8 9.5 %copy-start.12 = (s32[1,4]{1,0:T(1,128)S(1)}, s32[1,4]{1,0:T(1,128)}, u32[]{:S(2)}) copy-start(s32[1,4]{1,0:T(1,128)} %param.6) | copy-start | bytes 52
  47.1 8.8 %all-to-all-start.1 = ((f32[4,4,4]{0,2,1:T(4,128)}), f32[4,4,4]{0,2,1:T(4,128)S(1)}, u32[]{:S(2)}, u32[]{:S(2)}) async-start(f32[4,4,4]{0,2,1:T(4,128)} %fusion.5), calls=%async_computation.1 | async-start | bytes 16384 | tf_op jit(solution)/shard_map/all_to_all | solution.py:57
  51.3 37.2 %reduce-scatter.2.cloned.1.call-start = ((), (), s32[]{:S(2)}) async-start(), calls=%async_computation.3 | async-start | bytes 327680 | tf_op jit(solution)/shard_map/reduce_scatter | solution.py:60
  56.8 2.2 %copy-start.2 = (f32[512,2048]{1,0:T(8,128)S(1)}, f32[512,2048]{1,0:T(8,128)}, u32[]{:S(2)}) copy-start(f32[512,2048]{1,0:T(8,128)} %convolution_multiply_fusion) | copy-start | bytes 12582916
  56.8 3.5 %copy-start.4 = (f32[64,8,4,512]{3,1,2,0:T(8,128)S(1)}, f32[64,8,4,512]{3,1,2,0:T(8,128)}, u32[]{:S(2)}) copy-start(f32[64,8,4,512]{3,1,2,0:T(8,128)} %copy.21) | copy-start | bytes 12582916
  60.3 2.9 %copy-start.7 = (bf16[2048,128]{1,0:T(8,128)(2,1)S(1)}, bf16[2048,128]{1,0:T(8,128)(2,1)}, u32[]{:S(2)}) copy-start(bf16[2048,128]{1,0:T(8,128)(2,1)} %copy-done.6) | copy-start | bytes 1572868
  61.9 1.4 copy-start.3
  64.7 82.7 %all-reduce.3.cloned.1.call-start = ((), (), s32[]{:S(2)}) async-start(), calls=%async_computation.4 | async-start | bytes 786432 | tf_op jit(solution)/shard_map/psum | solution.py:68
  67.0 1.0 copy-start.5
  90.5 103.0 %all-reduce.5.cloned.1.call-start = ((), (), s32[]{:S(2)}) async-start(), calls=%async_computation.5 | async-start | bytes 786432 | tf_op jit(solution)/shard_map/psum | solution.py:68
Sparse Core Ops, SparseCore 0:
  64.8 23.6 reduce-scatter.1
  91.4 55.8 all-reduce.2
  150.3 43.1 all-reduce.4
